TPU v7x, 32 devices: a whole 2x2x4 slice. The times are simulated.
32 devices in a mesh: dp: 4 (over x, core), mp: 8 (over z, y).
Axes of the slice: x: 2, y: 2, z: 4, core: 2. Of those that a mesh axis runs over, the one named last changes fastest.
Arguments:
- source_prompts: bfloat16 [128, 64, 4096], P(None, None, 'mp'), may hold values from -6 to 6
- task_logits: float32 [8, 128], replicated, may hold values from -8 to 260
- task_ids: int32 [32], P('dp'), may hold values from 0 to 7
- key_weight: bfloat16 [4096, 4096], P(None, 'mp'), may hold values from -0.09375 to 0.09375
- value_weight: bfloat16 [4096, 4096], P(None, 'mp'), may hold values from -0.09375 to 0.09375
- queries: bfloat16 [32, 128, 4096], P(('dp', 'mp')), may hold values from -32 to 32
- keys: bfloat16 [32, 128, 4096], P(('dp', 'mp')), may hold values from -16 to 16
- values: bfloat16 [32, 128, 4096], P(('dp', 'mp')), may hold values from -6 to 6
- cotangent: bfloat16 [32, 128, 4096], P(('dp', 'mp')), may hold values from -6 to 6
Outputs:
- attended: bfloat16 [32, 128, 4096], P(('dp', 'mp'))
- source_grad: float32 [128, 64, 4096], P(None, 'dp', 'mp')
- logits_grad: float32 [8, 128], replicated
All inputs are finite; a program needn't handle non-finite values.
Results may differ from a plain program's by a relative error of at most 0.011.
Values may be sent and summed in bfloat16 or wider, within the bound.
A program may use at most 128 MiB of HBM per device.

v0:
```python
import jax
import jax.numpy as jnp
from jax import lax
from jax.sharding import PartitionSpec as P

D = 4096
HEADS = 32
DH = 128
NSRC = 128
NTASK = 8
PTOK = 64
SEQ = 128
E_DEV = 1
mask_fill = -1e30


def example_block(prompt_pair, queries, keys, values, cotangent):
    examples = queries.shape[0]
    score_scale = DH ** (-0.5)
    key_all = jnp.concatenate([prompt_pair[:, :, 0, :], keys], axis=1)
    value_all = jnp.concatenate([prompt_pair[:, :, 1, :], values], axis=1)
    query_heads = queries.reshape(examples, SEQ, HEADS, DH)
    key_heads = key_all.reshape(examples, PTOK + SEQ, HEADS, DH)
    value_heads = value_all.reshape(examples, PTOK + SEQ, HEADS, DH)
    cot_heads = cotangent.reshape(examples, SEQ, HEADS, DH)
    scores = (
        jnp.einsum("eihd,ejhd->ehij", query_heads, key_heads, preferred_element_type=jnp.float32)
        * score_scale
    )
    column = jnp.arange(PTOK + SEQ)[None, :]
    position = jnp.arange(SEQ)[:, None]
    visible = (column < PTOK) | (column - PTOK <= position)
    scores = jnp.where(visible[None, None], scores, mask_fill)
    top_score = jnp.max(scores, axis=3, keepdims=True)
    exponent = jnp.exp(scores - top_score)
    attention = exponent / jnp.sum(exponent, axis=3, keepdims=True)
    attention_rounded = attention.astype(jnp.bfloat16)
    attended = jnp.einsum(
        "ehij,ejhd->eihd", attention_rounded, value_heads, preferred_element_type=jnp.float32
    )
    attended = attended.astype(jnp.bfloat16).reshape(examples, SEQ, D)
    grad_attention = jnp.einsum(
        "eihd,ejhd->ehij", cot_heads, value_heads, preferred_element_type=jnp.float32
    )
    inner_sum = jnp.sum(attention * grad_attention, axis=3, keepdims=True)
    grad_scores = (attention * (grad_attention - inner_sum)).astype(jnp.bfloat16)
    key_grads = jnp.einsum(
        "ehij,eihd->ejhd",
        grad_scores[:, :, :, :PTOK],
        query_heads,
        preferred_element_type=jnp.float32,
    )
    key_grads = (key_grads * score_scale).astype(jnp.bfloat16).reshape(examples, PTOK, D)
    value_grads = jnp.einsum(
        "ehij,eihd->ejhd",
        attention_rounded[:, :, :, :PTOK],
        cot_heads,
        preferred_element_type=jnp.float32,
    )
    value_grads = value_grads.astype(jnp.bfloat16).reshape(examples, PTOK, D)
    return (attended, jnp.stack([key_grads, value_grads], axis=2))


def tile_products(tile_grad, source_prompts, mix_weights, col_width):
    rows_here = tile_grad.shape[1]
    own_prompts = lax.dynamic_slice_in_dim(
        source_prompts, lax.axis_index("dp") * rows_here, rows_here, 1
    )
    tile_flat = tile_grad.reshape(NTASK, rows_here * col_width)
    source_grad = jnp.dot(mix_weights.T, tile_flat, precision=lax.Precision.HIGHEST)
    source_grad = source_grad.reshape(NSRC, rows_here, col_width)
    weight_part = jnp.dot(
        tile_flat,
        own_prompts.reshape(NSRC, rows_here * col_width).astype(jnp.float32).T,
        precision=lax.Precision.HIGHEST,
    )
    return (source_grad, weight_part)


def on_device(
    source_prompts,
    task_logits,
    task_ids,
    key_weight,
    value_weight,
    queries,
    keys,
    values,
    cotangent,
):
    col_width = key_weight.shape[1]
    group_examples = task_ids.shape[0]
    mix_weights = jax.nn.softmax(task_logits, axis=1)
    mix_rounded = mix_weights.astype(jnp.bfloat16)
    mixture = jnp.dot(
        mix_rounded,
        source_prompts.reshape(NSRC, PTOK * col_width),
        preferred_element_type=jnp.float32,
    )
    mixture = mixture.astype(jnp.bfloat16).reshape(NTASK, PTOK, col_width)
    pair_weight = jnp.concatenate([key_weight, value_weight], axis=1)
    portion = lax.all_gather(mixture, "mp", axis=2, tiled=True)
    portion_rows = portion.reshape(NTASK * PTOK, portion.shape[2])
    projected = jnp.dot(portion_rows, pair_weight, preferred_element_type=jnp.float32)
    projected = projected.astype(jnp.bfloat16).reshape(NTASK, PTOK, 2, col_width)
    task_range = jnp.arange(NTASK, dtype=jnp.int32)
    selector_all = (task_ids[:, None] == task_range[None, :]).astype(jnp.bfloat16)
    table_full = lax.all_gather(projected, "mp", axis=3, tiled=True)
    own_offset = lax.axis_index("mp") * E_DEV
    own_selector = lax.dynamic_slice_in_dim(selector_all, own_offset, E_DEV, 0)
    chosen = jnp.dot(
        own_selector, table_full.reshape(NTASK, PTOK * 2 * D), preferred_element_type=jnp.float32
    )
    prompt_pair = chosen.astype(jnp.bfloat16).reshape(E_DEV, PTOK, 2, D)
    attended, outgoing_grads = example_block(prompt_pair, queries, keys, values, cotangent)
    incoming = lax.all_to_all(outgoing_grads, "mp", split_axis=3, concat_axis=0, tiled=True)
    group_grads = jnp.dot(
        selector_all.T,
        incoming.reshape(group_examples, PTOK * 2 * col_width),
        preferred_element_type=jnp.float32,
    )
    pair_weight_t = pair_weight.astype(jnp.float32).T
    task_rows = lax.psum_scatter(
        group_grads.reshape(NTASK, PTOK, 2 * col_width), "dp", scatter_dimension=1, tiled=True
    )
    rows_here = task_rows.shape[1]
    row_terms = jnp.dot(
        task_rows.reshape(NTASK * rows_here, 2 * col_width),
        pair_weight_t,
        precision=lax.Precision.HIGHEST,
    ).reshape(NTASK, rows_here, D)
    tile_grad = lax.psum_scatter(row_terms, "mp", scatter_dimension=2, tiled=True)
    source_grad, weight_part = tile_products(tile_grad, source_prompts, mix_weights, col_width)
    weight_grad = lax.psum(weight_part, ("dp", "mp"))
    logits_grad = mix_weights * (
        weight_grad - jnp.sum(mix_weights * weight_grad, axis=1, keepdims=True)
    )
    return (attended, source_grad, logits_grad)


def solution(mesh):
    placed = (
        P(None, None, "mp"),
        P(),
        P("dp"),
        P(None, "mp"),
        P(None, "mp"),
        P(("dp", "mp"), None, None),
        P(("dp", "mp"), None, None),
        P(("dp", "mp"), None, None),
        P(("dp", "mp"), None, None),
    )
    return jax.shard_map(
        on_device,
        mesh=mesh,
        in_specs=placed,
        out_specs=(P(("dp", "mp"), None, None), P(None, "dp", "mp"), P()),
        check_vma=False,
    )
```

profile of v0, /device:TPU:0, one launch (start us, length us, event | category | flops | bytes accessed | tf_op | source)
XLA Modules:
  0.0 497.0 jit_solution(17414920822181697347)
XLA Ops:
  7.2 0.8 reduce_max.18
  8.0 0.9 fusion.44
  8.9 12.5 %copy.91 = bf16[16,8,64,512]{3,1,2,0:T(8,128)(2,1)} copy(bf16[16,8,64,512]{3,2,1,0:T(8,128)(2,1)} %bitcast.125) | data formatting | bytes 16777216
  21.4 4.6 convolution_convert_fusion
  26.0 1.0 copy.63
  27.0 4.7 constant_dynamic-update-slice_fusion.1
  31.7 2.3 constant_dynamic-update-slice_fusion
  34.0 70.5 %all-gather.3.cloned.1.call-done = bf16[8,64,4096]{2,1,0:T(8,128)(2,1)} async-done(((bf16[8,64,512]{2,1,0:T(8,128)(2,1)}), bf16[8,64,4096]{2,1,0:T(8,128)(2,1)}) %all-gather.3.cloned.1.call-update) | async-done | bytes 4194320 | tf_op jit(solution)/shard_map/all_gather | solution.py:102
  104.5 9.1 %convolution_convert_fusion.1 = bf16[512,1024]{1,0:T(8,128)(2,1)S(1)} fusion(bf16[512,4096]{1,0:T(8,128)(2,1)} %bitcast.147, bf16[4096,1024]{1,0:T(8,128)(2,1)} %constant_dynamic-update-slice_fusion), kind=kOutput, calls=%fused_computation.30 | convolution fusion | flops 4295491584 | bytes 13631488 | tf_op jit(solution)/shard_map/dot_general | solution.py:104
  113.7 1.6 reshape.180
  115.3 0.2 reduce-scatter.3.cloned.1.call-start
  115.5 1.2 copy.94
  116.7 0.7 copy.67
  117.4 1.3 copy.69
  118.7 0.7 copy.64
  119.3 1.4 copy.73
  120.7 1.6 copy.95
  122.4 0.1 fusion.38
  122.5 116.0 %all-gather.5.cloned.1.call-done = bf16[8,64,2,4096]{3,2,1,0:T(2,128)(2,1)} async-done(((bf16[8,64,2,512]{3,2,1,0:T(2,128)(2,1)}), bf16[8,64,2,4096]{3,2,1,0:T(2,128)(2,1)}) %all-gather.5.cloned.1.call-update) | async-done | bytes 8388624 | tf_op jit(solution)/shard_map/all_gather | solution.py:108
  238.5 13.0 %reshape.181 = bf16[8,524288]{1,0:T(8,128)(2,1)} reshape(bf16[8,64,2,4096]{3,2,1,0:T(2,128)(2,1)} %all-gather.5.cloned.1.call-done) | data formatting | bytes 16777216 | tf_op jit(solution)/shard_map/reshape | solution.py:112
  251.5 5.7 %fusion.46 = f32[1,524288]{1,0:T(1,128)S(1)} fusion(bf16[8,524288]{1,0:T(8,128)(2,1)} %reshape.181, pred[8,8]{1,0:T(8,128)(4,1)S(1)} %iota_compare_fusion.1, s32[]{:T(128)S(6)} %select_n.11), kind=kOutput, calls=%fused_computation.69 | convolution fusion | flops 8388608 | bytes 10486276 | tf_op jit(solution)/shard_map/dot_general | solution.py:111
  257.2 1.1 convert_element_type.64
  258.3 1.3 reshape.182
  259.7 5.6 %slice_reduce_fusion = (bf16[64,4096]{1,0:T(8,128)(2,1)S(1)}, bf16[64,4096]{1,0:T(8,128)(2,1)S(1)}) fusion(bf16[1,64,2,4096]{3,2,1,0:T(2,128)(2,1)S(1)} %reshape.182), kind=kLoop, calls=%fused_computation.40 | loop fusion | bytes 2097152 | tf_op jit(solution)/shard_map/slice | solution.py:20
  265.4 0.2 copy.68
  265.6 0.1 copy_bitcast_fusion
  265.8 0.8 fusion.12
  266.6 0.9 fusion.57
  267.5 1.5 convert_bitcast_fusion
  269.0 0.5 copy-done.4
  269.5 0.9 fusion.15
  270.4 0.8 fusion.22
  271.2 0.6 fusion.27
  271.7 0.3 copy.76
  272.1 0.2 stack_reshape.6
  272.3 1.6 fusion.26
  273.9 0.3 copy.78
  274.3 0.2 stack_reshape.7
  274.5 1.1 pad_maximum_fusion
  275.6 5.0 %copy.79 = bf16[1,64,2,4096]{1,2,0,3:T(2,128)(2,1)S(1)} copy(bf16[1,64,2,4096]{3,1,2,0:T(8,128)(2,1)} %pad_maximum_fusion) | data formatting | bytes 2097152 | tf_op jit(solution)/shard_map/stack | solution.py:61
  280.6 2.7 reshape.201
  283.3 29.5 %all_to_all.15 = bf16[8,2,32768]{2,1,0:T(2,128)(2,1)} all-to-all(bf16[8,2,32768]{2,1,0:T(2,128)(2,1)} %reshape.201), channel_id=1, replica_groups=mesh['dp'=4,'mp'=8] {'mp'}, dimensions={0} | all-to-all | bytes 2097152 | tf_op jit(solution)/shard_map/all_to_all | solution.py:116
  312.8 3.1 reshape.202
  315.9 3.6 copy.80
  319.5 2.0 reshape.190
  321.6 1.9 fusion.41
  323.5 0.4 reduce-scatter.5.cloned.1.call-start
  323.9 29.9 %reduce-scatter.3.cloned.1.call-done = f32[8,16,1024]{2,0,1:T(8,128)} async-done(((f32[8,64,1024]{2,0,1:T(8,128)}), f32[8,16,1024]{2,0,1:T(8,128)}) %reduce-scatter.3.cloned.1.call-update) | async-done | bytes 524304 | tf_op jit(solution)/shard_map/reduce_scatter | solution.py:123
  353.8 13.3 %fusion.2 = f32[8,16,4096]{2,1,0:T(8,128)} fusion(bf16[4096,1024]{1,0:T(8,128)(2,1)} %constant_dynamic-update-slice_fusion, f32[8,16,1024]{2,0,1:T(8,128)} %reduce-scatter.3.cloned.1.call-done), kind=kOutput, calls=%fused_computation.3 | convolution fusion | flops 6442450944 | bytes 11010048 | tf_op jit(solution)/shard_map/dot_general | solution.py:127
  367.2 1.3 copy.66
  368.5 1.9 constant_dynamic-slice_fusion
  370.4 0.1 copy.92
  370.5 0.2 copy.65
  370.8 0.4 copy-done.7
  371.2 0.3 copy-done.11
  371.5 0.8 fusion.23
  372.3 1.3 copy.85
  373.6 62.5 %reduce-scatter.5.cloned.1.call-done = f32[8,16,512]{2,1,0:T(8,128)} async-done(((f32[8,16,4096]{2,1,0:T(8,128)}), f32[8,16,512]{2,1,0:T(8,128)}) %reduce-scatter.5.cloned.1.call-update) | async-done | bytes 262160 | tf_op jit(solution)/shard_map/reduce_scatter | solution.py:132
  436.2 4.6 fusion.28
  440.8 39.7 %psum.7 = f32[8,128]{1,0:T(8,128)S(1)} all-reduce(f32[8,128]{1,0:T(8,128)S(1)} %fusion.28), channel_id=1, replica_groups=mesh['dp'=4,'mp'=8] {'dp','mp'}, use_global_device_ids=true, to_apply=%region_7.8 | all-reduce | flops 1024 | bytes 8192 | tf_op jit(solution)/shard_map/psum | solution.py:134
  480.5 0.2 multiply_reduce_fusion
  480.7 0.7 subtract_multiply_fusion
  481.4 4.5 fusion.39
  485.9 4.4 copy.86
  (35 shorter events, 0.4 us)
Async XLA Ops:
  7.2 97.3 %all-gather.3.cloned.1.call-start = ((), (), s32[]{:S(2)}) async-start(), calls=%async_computation.3 | async-start | bytes 4718592 | tf_op jit(solution)/shard_map/all_gather | solution.py:102
  8.9 12.5 %copy-start.12 = (f32[8,128]{1,0:T(8,128)S(1)}, f32[8,128]{1,0:T(8,128)}, u32[]{:S(2)}) copy-start(f32[8,128]{1,0:T(8,128)} %param.10) | copy-start | bytes 12292
  27.0 211.6 %all-gather.5.cloned.1.call-start = ((), (), s32[]{:S(2)}) async-start(), calls=%async_computation.4 | async-start | bytes 9437184 | tf_op jit(solution)/shard_map/all_gather | solution.py:108
  27.0 4.7 copy-start.2
  113.6 1.9 copy-start.8
  113.6 3.1 copy-start.9
  115.3 238.6 %reduce-scatter.3.cloned.1.call-start = ((), (), s32[]{:S(2)}) async-start(), calls=%async_computation.5 | async-start | bytes 2621440 | tf_op jit(solution)/shard_map/reduce_scatter | solution.py:123
  115.5 3.2 copy-start.10
  118.7 3.7 copy-start.13
  259.6 6.1 %copy-start.3 = (bf16[16,8,32,128]{3,2,1,0:T(8,128)(2,1)S(1)}, bf16[16,8,32,128]{3,2,1,0:T(8,128)(2,1)}, u32[]{:S(2)}) copy-start(bf16[16,8,32,128]{3,2,1,0:T(8,128)(2,1)} %copy.94) | copy-start | bytes 3145732
  259.6 6.1 %copy-start.5 = (bf16[1,128,32,128]{3,1,2,0:T(8,128)(2,1)S(1)}, bf16[1,128,32,128]{3,1,2,0:T(8,128)(2,1)}, u32[]{:S(2)}) copy-start(bf16[1,128,32,128]{3,1,2,0:T(8,128)(2,1)} %copy.69) | copy-start | bytes 3145732
  265.3 1.3 copy-start
  267.5 2.9 copy-start.6
  267.5 2.0 copy-start.4
  323.5 112.7 %reduce-scatter.5.cloned.1.call-start = ((), (), s32[]{:S(2)}) async-start(), calls=%async_computation.6 | async-start | bytes 2359296 | tf_op jit(solution)/shard_map/reduce_scatter | solution.py:132
  368.5 1.9 copy-start.1
  368.5 2.7 copy-start.7
  368.5 3.0 copy-start.11
Sparse Core Ops, SparseCore 0:
  27.1 77.3 all-gather.2
  115.4 123.1 all-gather.4
  323.6 30.1 reduce-scatter.2
  367.3 68.8 reduce-scatter.4
where the time goes:
time: 506 us; the launch traced here: 497 us
  waiting for transfers between devices  279 us (55%)
  local copies, waits for them, and re-layouts  77.2 us (15%)
  blocking collectives  69.3 us (14%)
  matrix products  48.5 us (10%)
  between operations  14.3 us (3%)
  other arithmetic  8.09 us (2%)
    all_gather x1, waiting for transfers between devices, on_device(): table_full = lax.all_gather(projected, 'mp', axis=3, tiled=True)  116 us
    all_gather x1, waiting for transfers between devices, on_device(): portion = lax.all_gather(mixture, 'mp', axis=2, tiled=True)  70.5 us
    reduce_scatter x1, waiting for transfers between devices, on_device(): lax.psum_scatter(row_terms, 'mp', scatter_dimension=2, tiled=True)  62.5 us
    psum x1, blocking collectives, on_device(): weight_grad = lax.psum(weight_part, ('dp', 'mp'))  39.7 us
    unnamed x40, local copies, waits for them, and re-layouts  34.1 us
    reduce_scatter x1, waiting for transfers between devices, on_device(): lax.psum_scatter(group_grads.reshape(NTASK, PTOK, 2 * col_width), 'dp', s...  29.9 us
    all_to_all x1, blocking collectives, on_device(): lax.all_to_all(outgoing_grads, 'mp', split_axis=3, concat_axis=0, tiled=T...  29.5 us
    dot_general x1, matrix products, on_device(): jnp.dot(task_rows.reshape(NTASK * rows_here, 2 * col_width), pair_weight_...  13.3 us
  transfers between devices with their start and end apart: 4, of which 4 were waited for; matrix products, arithmetic and copies ran while one was open for 4% of the time, Pallas kernels for 0%

commit v1 on v0

--- a/solution.py
+++ b/solution.py
@@ -131,7 +131,7 @@
     ).reshape(NTASK, rows_here, D)
     tile_grad = lax.psum_scatter(row_terms, "mp", scatter_dimension=2, tiled=True)
     source_grad, weight_part = tile_products(tile_grad, source_prompts, mix_weights, col_width)
-    weight_grad = lax.psum(weight_part, ("dp", "mp"))
+    weight_grad = jnp.sum(lax.all_gather(weight_part, ("dp", "mp")), axis=0)
     logits_grad = mix_weights * (
         weight_grad - jnp.sum(mix_weights * weight_grad, axis=1, keepdims=True)
     )

time: 506 us -> 532 us (1.051)
  blocking collectives: 69.3 us -> 94.7 us
    all_gather x0 -> x1, blocking collectives: none -> 65.2 us  [on_device(): weight_grad = jnp.sum(lax.all_gather(weight_part, ('dp', 'mp')), axis=0)]
    psum x1 -> x0, blocking collectives: 39.7 us -> none  [on_device(): weight_grad = lax.psum(weight_part, ('dp', 'mp'))]
where the time goes in v1:
time: 532 us; the launch traced here: 522 us
  waiting for transfers between devices  279 us (52%)
  blocking collectives  94.7 us (18%)
  local copies, waits for them, and re-layouts  77.2 us (15%)
  matrix products  48.5 us (9%)
  between operations  14.3 us (3%)
  other arithmetic  8.12 us (2%)
    all_gather x1, waiting for transfers between devices, on_device(): table_full = lax.all_gather(projected, 'mp', axis=3, tiled=True)  116 us
    all_gather x1, waiting for transfers between devices, on_device(): portion = lax.all_gather(mixture, 'mp', axis=2, tiled=True)  70.5 us
    all_gather x1, blocking collectives, on_device(): weight_grad = jnp.sum(lax.all_gather(weight_part, ('dp', 'mp')), axis=0)  65.2 us
    reduce_scatter x1, waiting for transfers between devices, on_device(): lax.psum_scatter(row_terms, 'mp', scatter_dimension=2, tiled=True)  62.5 us
    unnamed x40, local copies, waits for them, and re-layouts  34.1 us
    reduce_scatter x1, waiting for transfers between devices, on_device(): lax.psum_scatter(group_grads.reshape(NTASK, PTOK, 2 * col_width), 'dp', s...  29.9 us
    all_to_all x1, blocking collectives, on_device(): lax.all_to_all(outgoing_grads, 'mp', split_axis=3, concat_axis=0, tiled=T...  29.5 us
    dot_general x1, matrix products, on_device(): jnp.dot(task_rows.reshape(NTASK * rows_here, 2 * col_width), pair_weight_...  13.3 us
  transfers between devices with their start and end apart: 4, of which 4 were waited for; matrix products, arithmetic and copies ran while one was open for 4% of the time, Pallas kernels for 0%

profile of v1, /device:TPU:0, one launch (start us, length us, event | category | flops | bytes accessed | tf_op | source)
XLA Modules:
  0.0 522.5 jit_solution(756910834729387383)
XLA Ops:
  7.2 0.8 reduce_max.18
  8.0 0.9 fusion.44
  8.9 12.5 %copy.91 = bf16[16,8,64,512]{3,1,2,0:T(8,128)(2,1)} copy(bf16[16,8,64,512]{3,2,1,0:T(8,128)(2,1)} %bitcast.127) | data formatting | bytes 16777216
  21.4 4.6 convolution_convert_fusion
  26.0 1.0 copy.63
  27.0 4.7 constant_dynamic-update-slice_fusion.1
  31.7 2.3 constant_dynamic-update-slice_fusion
  34.0 70.5 %all-gather.4.cloned.1.call-done = bf16[8,64,4096]{2,1,0:T(8,128)(2,1)} async-done(((bf16[8,64,512]{2,1,0:T(8,128)(2,1)}), bf16[8,64,4096]{2,1,0:T(8,128)(2,1)}) %all-gather.4.cloned.1.call-update) | async-done | bytes 4194320 | tf_op jit(solution)/shard_map/all_gather | solution.py:102
  104.5 9.1 %convolution_convert_fusion.1 = bf16[512,1024]{1,0:T(8,128)(2,1)S(1)} fusion(bf16[512,4096]{1,0:T(8,128)(2,1)} %bitcast.149, bf16[4096,1024]{1,0:T(8,128)(2,1)} %constant_dynamic-update-slice_fusion), kind=kOutput, calls=%fused_computation.30 | convolution fusion | flops 4295491584 | bytes 13631488 | tf_op jit(solution)/shard_map/dot_general | solution.py:104
  113.7 1.6 reshape.180
  115.3 0.2 reduce-scatter.3.cloned.1.call-start
  115.5 1.2 copy.94
  116.7 0.7 copy.67
  117.4 1.3 copy.69
  118.7 0.7 copy.64
  119.3 1.4 copy.73
  120.7 1.6 copy.95
  122.4 0.1 fusion.38
  122.5 116.0 %all-gather.6.cloned.1.call-done = bf16[8,64,2,4096]{3,2,1,0:T(2,128)(2,1)} async-done(((bf16[8,64,2,512]{3,2,1,0:T(2,128)(2,1)}), bf16[8,64,2,4096]{3,2,1,0:T(2,128)(2,1)}) %all-gather.6.cloned.1.call-update) | async-done | bytes 8388624 | tf_op jit(solution)/shard_map/all_gather | solution.py:108
  238.5 13.0 %reshape.181 = bf16[8,524288]{1,0:T(8,128)(2,1)} reshape(bf16[8,64,2,4096]{3,2,1,0:T(2,128)(2,1)} %all-gather.6.cloned.1.call-done) | data formatting | bytes 16777216 | tf_op jit(solution)/shard_map/reshape | solution.py:112
  251.5 5.7 %fusion.46 = f32[1,524288]{1,0:T(1,128)S(1)} fusion(bf16[8,524288]{1,0:T(8,128)(2,1)} %reshape.181, pred[8,8]{1,0:T(8,128)(4,1)S(1)} %iota_compare_fusion.1, s32[]{:T(128)S(6)} %select_n.11), kind=kOutput, calls=%fused_computation.70 | convolution fusion | flops 8388608 | bytes 10486276 | tf_op jit(solution)/shard_map/dot_general | solution.py:111
  257.2 1.1 convert_element_type.64
  258.3 1.3 reshape.182
  259.7 5.6 %slice_reduce_fusion = (bf16[64,4096]{1,0:T(8,128)(2,1)S(1)}, bf16[64,4096]{1,0:T(8,128)(2,1)S(1)}) fusion(bf16[1,64,2,4096]{3,2,1,0:T(2,128)(2,1)S(1)} %reshape.182), kind=kLoop, calls=%fused_computation.40 | loop fusion | bytes 2097152 | tf_op jit(solution)/shard_map/slice | solution.py:20
  265.4 0.2 copy.68
  265.6 0.1 copy_bitcast_fusion
  265.8 0.8 fusion.12
  266.6 0.9 fusion.57
  267.5 1.5 convert_bitcast_fusion
  269.0 0.5 copy-done.4
  269.5 0.9 fusion.15
  270.4 0.8 fusion.22
  271.2 0.6 fusion.27
  271.7 0.3 copy.76
  272.1 0.2 stack_reshape.6
  272.3 1.6 fusion.26
  273.9 0.3 copy.78
  274.3 0.2 stack_reshape.7
  274.5 1.1 pad_maximum_fusion
  275.6 5.0 copy.79
  280.6 2.7 reshape.202
  283.3 29.5 %all_to_all.15 = bf16[8,2,32768]{2,1,0:T(2,128)(2,1)} all-to-all(bf16[8,2,32768]{2,1,0:T(2,128)(2,1)} %reshape.202), channel_id=1, replica_groups=mesh['dp'=4,'mp'=8] {'mp'}, dimensions={0} | all-to-all | bytes 2097152 | tf_op jit(solution)/shard_map/all_to_all | solution.py:116
  312.8 3.1 reshape.203
  315.9 3.6 copy.80
  319.5 2.0 reshape.190
  321.6 1.9 fusion.41
  323.5 0.4 reduce-scatter.5.cloned.1.call-start
  323.9 29.9 %reduce-scatter.3.cloned.1.call-done = f32[8,16,1024]{2,0,1:T(8,128)} async-done(((f32[8,64,1024]{2,0,1:T(8,128)}), f32[8,16,1024]{2,0,1:T(8,128)}) %reduce-scatter.3.cloned.1.call-update) | async-done | bytes 524304 | tf_op jit(solution)/shard_map/reduce_scatter | solution.py:123
  353.8 13.3 %fusion.2 = f32[8,16,4096]{2,1,0:T(8,128)} fusion(bf16[4096,1024]{1,0:T(8,128)(2,1)} %constant_dynamic-update-slice_fusion, f32[8,16,1024]{2,0,1:T(8,128)} %reduce-scatter.3.cloned.1.call-done), kind=kOutput, calls=%fused_computation.3 | convolution fusion | flops 6442450944 | bytes 11010048 | tf_op jit(solution)/shard_map/dot_general | solution.py:127
  367.2 1.3 copy.66
  368.5 1.9 constant_dynamic-slice_fusion
  370.4 0.1 copy.92
  370.5 0.2 copy.65
  370.8 0.4 copy-done.7
  371.2 0.3 copy-done.11
  371.5 0.8 fusion.23
  372.3 1.3 copy.85
  373.6 62.5 %reduce-scatter.5.cloned.1.call-done = f32[8,16,512]{2,1,0:T(8,128)} async-done(((f32[8,16,4096]{2,1,0:T(8,128)}), f32[8,16,512]{2,1,0:T(8,128)}) %reduce-scatter.5.cloned.1.call-update) | async-done | bytes 262160 | tf_op jit(solution)/shard_map/reduce_scatter | solution.py:132
  436.2 4.6 fusion.28
  440.8 65.2 %all-gather = f32[256,128]{1,0:T(8,128)S(1)} all-gather(f32[8,128]{1,0:T(8,128)S(1)} %fusion.28), channel_id=2, replica_groups=mesh['dp'=4,'mp'=8] {'dp','mp'}, dimensions={0}, use_global_device_ids=true | all-gather | bytes 135168 | tf_op jit(solution)/shard_map/all_gather | solution.py:134
  506.0 0.2 multiply_reduce_fusion
  506.1 0.7 subtract_multiply_fusion
  506.8 4.5 fusion.39
  511.3 4.4 copy.86
  (36 shorter events, 0.4 us)
Async XLA Ops:
  7.2 97.3 %all-gather.4.cloned.1.call-start = ((), (), s32[]{:S(2)}) async-start(), calls=%async_computation.3 | async-start | bytes 4718592 | tf_op jit(solution)/shard_map/all_gather | solution.py:102
  8.9 12.5 %copy-start.12 = (f32[8,128]{1,0:T(8,128)S(1)}, f32[8,128]{1,0:T(8,128)}, u32[]{:S(2)}) copy-start(f32[8,128]{1,0:T(8,128)} %param.10) | copy-start | bytes 12292
  27.0 211.6 %all-gather.6.cloned.1.call-start = ((), (), s32[]{:S(2)}) async-start(), calls=%async_computation.4 | async-start | bytes 9437184 | tf_op jit(solution)/shard_map/all_gather | solution.py:108
  27.0 4.7 copy-start.2
  113.6 1.9 copy-start.8
  113.6 3.1 copy-start.9
  115.3 238.6 %reduce-scatter.3.cloned.1.call-start = ((), (), s32[]{:S(2)}) async-start(), calls=%async_computation.5 | async-start | bytes 2621440 | tf_op jit(solution)/shard_map/reduce_scatter | solution.py:123
  115.5 3.2 copy-start.10
  118.7 3.7 copy-start.13
  259.6 6.1 %copy-start.3 = (bf16[16,8,32,128]{3,2,1,0:T(8,128)(2,1)S(1)}, bf16[16,8,32,128]{3,2,1,0:T(8,128)(2,1)}, u32[]{:S(2)}) copy-start(bf16[16,8,32,128]{3,2,1,0:T(8,128)(2,1)} %copy.94) | copy-start | bytes 3145732
  259.6 6.1 %copy-start.5 = (bf16[1,128,32,128]{3,1,2,0:T(8,128)(2,1)S(1)}, bf16[1,128,32,128]{3,1,2,0:T(8,128)(2,1)}, u32[]{:S(2)}) copy-start(bf16[1,128,32,128]{3,1,2,0:T(8,128)(2,1)} %copy.69) | copy-start | bytes 3145732
  265.3 1.3 copy-start
  267.5 2.9 copy-start.6
  267.5 2.0 copy-start.4
  323.5 112.7 %reduce-scatter.5.cloned.1.call-start = ((), (), s32[]{:S(2)}) async-start(), calls=%async_computation.6 | async-start | bytes 2359296 | tf_op jit(solution)/shard_map/reduce_scatter | solution.py:132
  368.5 1.9 copy-start.1
  368.5 2.7 copy-start.7
  368.5 3.0 copy-start.11
Sparse Core Ops, SparseCore 0:
  27.1 77.3 all-gather.3
  115.4 123.1 all-gather.5
  323.6 30.1 reduce-scatter.2
  367.3 68.8 reduce-scatter.4
